TPU v7x, 32 devices: a whole 2x2x4 slice. The times are simulated.
32 devices in a mesh: groups: 2 (over y), row: 8 (over z, x), col: 2 (over core).
Axes of the slice: x: 2, y: 2, z: 4, core: 2. Of those that a mesh axis runs over, the one named last changes fastest.
Arguments:
- teacher: bfloat16 [16384, 4096], P(('groups', 'row'), 'col'), parts along dimension 0, may hold values from -6 to 6
- proj_weight: bfloat16 [4096, 512], P('col'), may hold values from -0.09375 to 0.09375
- student: bfloat16 [512, 32, 512], P(('groups', 'col'), 'row'), parts along dimension 0, may hold values from -6 to 6
- dw_kernel: float32 [7, 7, 512], replicated, may hold values from -2 to 2
- dw_bias: float32 [512], replicated, may hold values from -4 to 4
- norm_gain: float32 [512], replicated, may hold values from 0.1 to 1.9
- norm_bias: float32 [512], replicated, may hold values from -4 to 4
- w_in: bfloat16 [512, 2048], replicated, may hold values from -0.25 to 0.25
- b_in: float32 [2048], replicated, may hold values from -4 to 4
- w_out: bfloat16 [2048, 512], replicated, may hold values from -0.125 to 0.125
- b_out: float32 [512], replicated, may hold values from -4 to 4
- layer_scale: float32 [512], replicated, may hold values from 0.25 to 1
Outputs:
- student_grad: float32 [512, 32, 512], P(('groups', 'col'), 'row'), parts along dimension 0
There are 2 independent parts, one for each index of `groups`. A program takes and returns all parts, laid end to end along the dimension named above; an argument that names none is the same for every part. Nothing has to cross between parts.
All inputs are finite; a program needn't handle non-finite values.
Results may differ from a plain program's by a relative error of at most 0.0044.
Values may be sent and summed in bfloat16 or wider, within the bound.
No kernel may reach another device: no remote copies, remote signals or barrier semaphores. Data moves between devices by JAX's collectives and lax.ppermute only.
A program may use at most 64 MiB of HBM per device.

v0:
```python
import jax
import jax.numpy as jnp
from jax import lax
from jax.sharding import PartitionSpec as P

NORM_EPSILON = 1e-06


def with_halo(block, sides, width):
    for axis, dim in sides:
        count = lax.axis_size(axis)
        forward = [(i, i + 1) for i in range(count - 1)]
        backward = [(target, source) for source, target in forward]
        low = lax.ppermute(
            lax.slice_in_dim(block, block.shape[dim] - width, None, axis=dim), axis, forward
        )
        high = lax.ppermute(lax.slice_in_dim(block, 0, width, axis=dim), axis, backward)
        block = jnp.concatenate([low, block, high], axis=dim)
    return block


def depthwise(padded, kernel, out_rows, out_cols):
    summed = jnp.zeros((out_rows, out_cols, padded.shape[2]), jnp.float32)
    for row_tap in range(7):
        for col_tap in range(7):
            window = padded[row_tap : row_tap + out_rows, col_tap : col_tap + out_cols].astype(
                jnp.float32
            )
            summed = summed + kernel[row_tap, col_tap] * window
    return summed


def gelu_slope(values):
    return (
        0.5 * (1.0 + lax.erf(values * 0.7071067811865476))
        + values * jnp.exp(-0.5 * values * values) * 0.3989422804014327
    )


def on_device(
    teacher,
    proj_weight,
    student,
    dw_kernel,
    dw_bias,
    norm_gain,
    norm_bias,
    w_in,
    b_in,
    w_out,
    b_out,
    layer_scale,
):
    row_count = lax.axis_size("row")
    tile_v, tile_u, channels = student.shape
    grid_u = tile_u * row_count
    local_lines = teacher.shape[0] // grid_u
    raw_tokens = teacher.reshape(local_lines, grid_u, teacher.shape[1])
    arrived = lax.all_to_all(raw_tokens, "row", split_axis=1, concat_axis=0, tiled=True)
    partial_value = jnp.dot(
        arrived.reshape(-1, arrived.shape[2]), proj_weight, preferred_element_type=jnp.float32
    )
    partial_value = partial_value.reshape(arrived.shape[0], tile_u, channels)
    target = lax.psum_scatter(partial_value, "col", scatter_dimension=0, tiled=True).astype(
        jnp.bfloat16
    )
    padded = with_halo(student, (("row", 1), ("col", 0)), 3)
    conv_out = depthwise(padded, dw_kernel, tile_v, tile_u) + dw_bias
    mean_val = jnp.mean(conv_out, axis=-1, keepdims=True)
    centred = conv_out - mean_val
    variance = jnp.mean(centred * centred, axis=-1, keepdims=True)
    inv_scale = lax.rsqrt(variance + NORM_EPSILON)
    normal_form = centred * inv_scale
    normed = (normal_form * norm_gain + norm_bias).astype(jnp.bfloat16).reshape(-1, channels)
    hidden_pre = jnp.dot(normed, w_in, preferred_element_type=jnp.float32) + b_in
    activated = jax.nn.gelu(hidden_pre, approximate=False).astype(jnp.bfloat16)
    branch = jnp.dot(activated, w_out, preferred_element_type=jnp.float32) + b_out
    branch = branch.reshape(tile_v, tile_u, channels)
    mismatch = student.astype(jnp.float32) + layer_scale * branch - target.astype(jnp.float32)
    d_branch = (layer_scale * mismatch).astype(jnp.bfloat16).reshape(-1, channels)
    d_activated = jnp.dot(d_branch, w_out.T, preferred_element_type=jnp.float32)
    d_hidden = (d_activated * gelu_slope(hidden_pre)).astype(jnp.bfloat16)
    d_normed = jnp.dot(d_hidden, w_in.T, preferred_element_type=jnp.float32).reshape(
        tile_v, tile_u, channels
    )
    scaled = d_normed * norm_gain
    d_conv_out = inv_scale * (
        scaled
        - jnp.mean(scaled, axis=-1, keepdims=True)
        - normal_form * jnp.mean(scaled * normal_form, axis=-1, keepdims=True)
    )
    d_padded = with_halo(d_conv_out, (("row", 1), ("col", 0)), 3)
    return mismatch + depthwise(d_padded, dw_kernel[::-1, ::-1], tile_v, tile_u)


def solution(mesh):
    placed = (
        P(("groups", "row"), "col"),
        P("col", None),
        P(("groups", "col"), "row", None),
        P(),
        P(),
        P(),
        P(),
        P(),
        P(),
        P(),
        P(),
        P(),
    )
    return jax.shard_map(
        on_device,
        mesh=mesh,
        in_specs=placed,
        out_specs=P(("groups", "col"), "row", None),
        check_vma=False,
    )
```

profile of v0, /device:TPU:11, one launch (start us, length us, event | category | flops | bytes accessed | tf_op | source)
XLA Modules:
  0.0 258.3 jit_solution(15804994926780199484)
XLA Ops:
  6.5 6.7 %copy.56 = bf16[32,32,2048]{2,0,1:T(8,128)(2,1)} copy(bf16[32,32,2048]{2,1,0:T(8,128)(2,1)} %bitcast.64) | data formatting | bytes 8388608 | tf_op jit(solution)/shard_map/reshape | solution.py:58
  13.2 5.8 %all-to-all-start = ((bf16[32,32,2048]{2,0,1:T(8,128)(2,1)}), bf16[32,32,2048]{2,0,1:T(8,128)(2,1)}, u32[]{:S(2)}, u32[]{:S(2)}) async-start(bf16[32,32,2048]{2,0,1:T(8,128)(2,1)} %copy.56), calls=%async_computation | async-start | bytes 8388608 | tf_op jit(solution)/shard_map/all_to_all | solution.py:59
  19.0 0.4 fusion.189
  19.4 0.1 copy.80
  19.5 3.1 %collective-permute-start = (bf16[128,3,512]{2,0,1:T(8,128)(2,1)S(1)}, bf16[128,3,512]{2,0,1:T(8,128)(2,1)S(1)}, u32[]{:S(2)}, u32[]{:S(2)}) collective-permute-start(bf16[128,3,512]{2,0,1:T(8,128)(2,1)S(1)} %copy.80), channel_id=1, source_target_pairs={{0,2},{2,4},{4,6},{6,8},{8,10},{10,12},{12,14},{1,3},{3,5},{5,7},{... | collective-permute-start | bytes 1179656 | tf_op jit(solution)/shard_map/ppermute | solution.py:14
  22.6 0.1 copy.81
  22.7 2.2 collective-permute-start.1
  25.0 93.0 %collective-permute-done = bf16[128,3,512]{2,0,1:T(8,128)(2,1)S(1)} collective-permute-done((bf16[128,3,512]{2,0,1:T(8,128)(2,1)S(1)}, bf16[128,3,512]{2,0,1:T(8,128)(2,1)S(1)}, u32[]{:S(2)}, u32[]{:S(2)}) %collective-permute-start) | collective-permute-done | bytes 393248 | tf_op jit(solution)/shard_map/ppermute | solution.py:14
  118.0 0.1 constant_dynamic-update-slice_fusion.4
  118.0 1.0 constant_dynamic-update-slice_fusion.3
  119.0 0.9 copy-done.4
  120.0 0.8 constant_dynamic-update-slice_fusion.5
  120.8 1.1 copy-done.7
  121.9 2.4 collective-permute-start.3
  124.3 1.3 collective-permute-start.2
  125.6 2.6 %copy.57 = bf16[8,32,4,2048]{3,1,0,2:T(8,128)(2,1)S(1)} copy(bf16[8,32,4,2048]{3,1,2,0:T(8,128)(2,1)} %bitcast.51) | data formatting | bytes 8388608 | tf_op jit(solution)/shard_map/all_to_all | solution.py:59
  128.3 0.2 copy-done.13
  128.5 3.7 %fusion.16 = f32[256,4,512]{2,0,1:T(8,128)} fusion(bf16[256,4,2048]{2,0,1:T(8,128)(2,1)S(1)} %bitcast.65, bf16[2048,512]{1,0:T(8,128)(2,1)S(1)} %copy-done.13), kind=kOutput, calls=%fused_computation.76 | convolution fusion | flops 2147483648 | bytes 8388608 | tf_op jit(solution)/shard_map/dot_general | solution.py:60
  132.2 0.0 reduce-scatter.2.cloned.1.call-update
  132.2 21.4 %fusion.185 = (f32[128,4]{0,1:T(4,128)S(1)}, f32[128,4,512]{2,0,1:T(8,128)S(1)}) fusion(f32[512]{0:T(512)S(1)} %copy-done.11, bf16[3,10,512]{2,0,1:T(4,128)(2,1)S(1)} %collective-permute-done.3, bf16[128,10,512]{2,0,1:T(8,128)(2,1)} %copy-done.7, f32[512]{0:T(512)S(1)} %bitcast.122, f32[512]{0:T(512)S(1)} %bitcast.124, f32[512]{0:T(512)S(1)} %bitcast.68, ...), kind=kLoop, calls=%fused_computation.343 | loop fusion | flops 71826944 | bytes 6195200 | tf_op jit(solution)/shard_map/reduce_sum | solution.py:69
  153.6 0.3 multiply_reduce_fusion.2
  153.9 0.2 add_convert_fusion
  154.2 1.2 copy.54
  155.4 2.0 reshape.52
  157.4 2.4 fusion.193
  159.8 1.9 copy-done.6
  161.8 10.1 %fusion.20 = f32[512,512]{1,0:T(8,128)} fusion(bf16[2048,512]{1,0:T(8,128)(2,1)S(1)} %copy-done.14, f32[512,2048]{1,0:T(8,128)S(1)} %fusion.193, f32[2048]{0:T(1024)S(1)} %copy-done.15, f32[512]{0:T(512)S(1)} %copy-done.16), kind=kOutput, calls=%fused_computation.79 | convolution fusion | flops 1143209984 | bytes 7350272 | tf_op jit(solution)/shard_map/dot_general | solution.py:77
  171.9 2.6 %reshape.53 = f32[128,4,512]{2,1,0:T(4,128)} reshape(f32[512,512]{1,0:T(8,128)} %fusion.20) | data formatting | bytes 2097152 | tf_op jit(solution)/shard_map/reshape | solution.py:78
  174.5 2.1 multiply_convert_fusion
  176.6 1.2 copy.58
  177.8 2.0 reshape.55
  179.8 7.0 %multiply_reduce_fusion.1 = (f32[512]{0:T(512)S(1)}, f32[512,512]{1,0:T(8,128)}) fusion(f32[512]{0:T(512)S(1)} %copy-done.9, bf16[512,2048]{1,0:T(8,128)(2,1)S(1)} %copy-done, f32[512,2048]{1,0:T(8,128)} %copy-done.6, bf16[512,512]{1,0:T(8,128)(2,1)} %reshape.55, bf16[2048,512]{1,0:T(8,128)(2,1)} %param.21, f32[2048]{0:T(1024)S(1)} %copy-done.15), kind=kOutput, calls=%fused_computation.216 | convolution fusion | flops 2159541760 | bytes 9973760 | tf_op jit(solution)/shard_map/dot_general | solution.py:83
  186.9 2.5 reshape.56
  189.4 1.7 multiply_reduce_fusion
  191.1 0.1 div.17
  191.2 0.1 copy.60
  191.3 1.7 subtract_multiply_fusion
  193.0 0.2 fusion.188
  193.2 1.9 collective-permute-start.5
  195.1 5.0 %collective-permute-start.4 = (f32[128,3,512]{2,0,1:T(8,128)S(1)}, f32[128,3,512]{2,0,1:T(8,128)S(1)}, u32[]{:S(2)}, u32[]{:S(2)}) collective-permute-start(f32[128,3,512]{2,0,1:T(8,128)S(1)} %get-tuple-element.13), channel_id=1, source_target_pairs={{0,2},{2,4},{4,6},{6,8},{8,10},{10,12},{12,14},{1,3},{3,5},{5,7},{... | collective-permute-start | bytes 2359304 | tf_op jit(solution)/shard_map/ppermute | solution.py:14
  200.1 26.2 %collective-permute-done.5 = f32[128,3,512]{2,0,1:T(8,128)S(1)} collective-permute-done((f32[128,3,512]{2,0,1:T(8,128)S(1)}, f32[128,3,512]{2,0,1:T(8,128)S(1)}, u32[]{:S(2)}, u32[]{:S(2)}) %collective-permute-start.5) | collective-permute-done | bytes 786464 | tf_op jit(solution)/shard_map/ppermute | solution.py:17
  226.3 6.7 %collective-permute-done.4 = f32[128,3,512]{2,0,1:T(8,128)S(1)} collective-permute-done((f32[128,3,512]{2,0,1:T(8,128)S(1)}, f32[128,3,512]{2,0,1:T(8,128)S(1)}, u32[]{:S(2)}, u32[]{:S(2)}) %collective-permute-start.4) | collective-permute-done | bytes 786464 | tf_op jit(solution)/shard_map/ppermute | solution.py:14
  233.1 1.4 collective-permute-start.6
  234.5 3.0 %collective-permute-start.7 = (f32[3,10,512]{2,0,1:T(4,128)S(1)}, f32[3,10,512]{2,0,1:T(4,128)S(1)}, u32[]{:S(2)}, u32[]{:S(2)}) collective-permute-start(f32[3,10,512]{2,0,1:T(4,128)S(1)} %get-tuple-element.10), channel_id=1, source_target_pairs={{1,0},{3,2},{5,4},{7,6},{9,8},{11,10},{13,12},{15,14},{17,16},{19,... | collective-permute-start | bytes 184328 | tf_op jit(solution)/shard_map/ppermute | solution.py:17
  237.6 0.9 collective-permute-done.7
  238.5 1.0 maximum_maximum_fusion
  239.6 10.3 %fusion.85 = f32[128,4,512]{2,0,1:T(8,128)S(1)} fusion(f32[131,10,512]{2,0,1:T(8,128)S(1)} %get-tuple-element.8, f32[128,3,512]{2,0,1:T(8,128)S(1)} %collective-permute-done.5, f32[128,4,512]{2,0,1:T(8,128)S(1)} %subtract_multiply_fusion, f32[128,3,512]{2,0,1:T(8,128)S(1)} %collective-permute-done.4, f32[131,10,512]{2,0,1:T(8,128)S(1)} %get-tuple-element.7, ...), kind=kLoop, calls=%fused_computation.145 | loop fusion | flops 28835840 | bytes 50434048 | tf_op jit(solution)/shard_map/add | solution.py:93
  249.9 1.6 copy.61
  (46 shorter events, 0.3 us)
Async XLA Ops:
  6.5 150.9 %copy-start = (bf16[512,2048]{1,0:T(8,128)(2,1)S(1)}, bf16[512,2048]{1,0:T(8,128)(2,1)}, u32[]{:S(2)}) copy-start(bf16[512,2048]{1,0:T(8,128)(2,1)} %param.19) | copy-start | bytes 6291460
  13.2 5.8 %copy-start.1 = (bf16[128,4,512]{2,1,0:T(4,128)(2,1)S(1)}, bf16[128,4,512]{2,1,0:T(4,128)(2,1)}, u32[]{:S(2)}) copy-start(bf16[128,4,512]{2,1,0:T(4,128)(2,1)} %param.14) | copy-start | bytes 1572868
  13.2 11.7 %copy-start.8 = (f32[7,7,512]{2,1,0:T(8,128)S(1)}, f32[7,7,512]{2,1,0:T(8,128)}, u32[]{:S(2)}) copy-start(f32[7,7,512]{2,1,0:T(8,128)} %param.15) | copy-start | bytes 301060
  13.2 112.4 %all-to-all-start = ((bf16[32,32,2048]{2,0,1:T(8,128)(2,1)}), bf16[32,32,2048]{2,0,1:T(8,128)(2,1)}, u32[]{:S(2)}, u32[]{:S(2)}) async-start(bf16[32,32,2048]{2,0,1:T(8,128)(2,1)} %copy.56), calls=%async_computation | async-start | bytes 8388608 | tf_op jit(solution)/shard_map/all_to_all | solution.py:59
  19.0 155.5 %reduce-scatter.2.cloned.1.call-start = ((), (), s32[]{:S(2)}) async-start(), calls=%async_computation.2 | async-start | bytes 3145728 | tf_op jit(solution)/shard_map/reduce_scatter | solution.py:64
  19.5 98.5 %collective-permute-start = (bf16[128,3,512]{2,0,1:T(8,128)(2,1)S(1)}, bf16[128,3,512]{2,0,1:T(8,128)(2,1)S(1)}, u32[]{:S(2)}, u32[]{:S(2)}) collective-permute-start(bf16[128,3,512]{2,0,1:T(8,128)(2,1)S(1)} %copy.80), channel_id=1, source_target_pairs={{0,2},{2,4},{4,6},{6,8},{8,10},{10,12},{12,14},{1,3},{3,5},{5,7},{... | collective-permute-start | bytes 1179656 | tf_op jit(solution)/shard_map/ppermute | solution.py:14
  22.7 97.3 %collective-permute-start.1 = (bf16[128,3,512]{2,0,1:T(8,128)(2,1)S(1)}, bf16[128,3,512]{2,0,1:T(8,128)(2,1)S(1)}, u32[]{:S(2)}, u32[]{:S(2)}) collective-permute-start(bf16[128,3,512]{2,0,1:T(8,128)(2,1)S(1)} %copy.81), channel_id=1, source_target_pairs={{2,0},{4,2},{6,4},{8,6},{10,8},{12,10},{14,12},{3,1},{5,3},{7,5},{... | collective-permute-start | bytes 1179656 | tf_op jit(solution)/shard_map/ppermute | solution.py:17
  119.0 0.9 copy-start.4
  120.8 1.1 copy-start.7
  121.9 10.3 %collective-permute-start.3 = (bf16[3,10,512]{2,0,1:T(4,128)(2,1)S(1)}, bf16[3,10,512]{2,0,1:T(4,128)(2,1)S(1)}, u32[]{:S(2)}, u32[]{:S(2)}) collective-permute-start(bf16[3,10,512]{2,0,1:T(4,128)(2,1)S(1)} %get-tuple-element.12), channel_id=1, source_target_pairs={{1,0},{3,2},{5,4},{7,6},{9,8},{11,10},{13,12},{15,14},{17,16},{19,... | collective-permute-start | bytes 92168 | tf_op jit(solution)/shard_map/ppermute | solution.py:17
  124.3 7.9 %collective-permute-start.2 = (bf16[3,10,512]{2,0,1:T(4,128)(2,1)S(1)}, bf16[3,10,512]{2,0,1:T(4,128)(2,1)S(1)}, u32[]{:S(2)}, u32[]{:S(2)}) collective-permute-start(bf16[3,10,512]{2,0,1:T(4,128)(2,1)S(1)} %get-tuple-element.11), channel_id=1, source_target_pairs={{0,1},{2,3},{4,5},{6,7},{8,9},{10,11},{12,13},{14,15},{16,17},{18,... | collective-permute-start | bytes 92168 | tf_op jit(solution)/shard_map/ppermute | solution.py:14
  125.6 2.9 %copy-start.13 = (bf16[2048,512]{1,0:T(8,128)(2,1)S(1)}, bf16[2048,512]{1,0:T(8,128)(2,1)}, u32[]{:S(2)}) copy-start(bf16[2048,512]{1,0:T(8,128)(2,1)} %param.13) | copy-start | bytes 6291460
  128.5 3.7 %copy-start.11 = (f32[512]{0:T(512)S(1)}, f32[512]{0:T(512)}, u32[]{:S(2)}) copy-start(f32[512]{0:T(512)} %param.16) | copy-start | bytes 6148
  132.2 21.7 %copy-start.9 = (f32[512]{0:T(512)S(1)}, f32[512]{0:T(512)}, u32[]{:S(2)}) copy-start(f32[512]{0:T(512)} %param.17) | copy-start | bytes 6148
  132.2 21.7 %copy-start.12 = (f32[512]{0:T(512)S(1)}, f32[512]{0:T(512)}, u32[]{:S(2)}) copy-start(f32[512]{0:T(512)} %param.18) | copy-start | bytes 6148
  155.4 6.4 %copy-start.15 = (f32[2048]{0:T(1024)S(1)}, f32[2048]{0:T(1024)}, u32[]{:S(2)}) copy-start(f32[2048]{0:T(1024)} %param.20) | copy-start | bytes 24580
  155.4 6.4 %copy-start.16 = (f32[512]{0:T(512)S(1)}, f32[512]{0:T(512)}, u32[]{:S(2)}) copy-start(f32[512]{0:T(512)} %param.22) | copy-start | bytes 6148
  157.4 4.4 %copy-start.14 = (bf16[2048,512]{1,0:T(8,128)(2,1)S(1)}, bf16[2048,512]{1,0:T(8,128)(2,1)}, u32[]{:S(2)}) copy-start(bf16[2048,512]{1,0:T(8,128)(2,1)} %param.21) | copy-start | bytes 6291460
  159.8 1.9 copy-start.6
  161.8 12.7 %copy-start.10 = (f32[512]{0:T(512)S(1)}, f32[512]{0:T(512)}, u32[]{:S(2)}) copy-start(f32[512]{0:T(512)} %param.23) | copy-start | bytes 6148
  193.2 33.1 %collective-permute-start.5 = (f32[128,3,512]{2,0,1:T(8,128)S(1)}, f32[128,3,512]{2,0,1:T(8,128)S(1)}, u32[]{:S(2)}, u32[]{:S(2)}) collective-permute-start(f32[128,3,512]{2,0,1:T(8,128)S(1)} %get-tuple-element.14), channel_id=1, source_target_pairs={{2,0},{4,2},{6,4},{8,6},{10,8},{12,10},{14,12},{3,1},{5,3},{7,5},{... | collective-permute-start | bytes 2359304 | tf_op jit(solution)/shard_map/ppermute | solution.py:17
  195.1 37.9 %collective-permute-start.4 = (f32[128,3,512]{2,0,1:T(8,128)S(1)}, f32[128,3,512]{2,0,1:T(8,128)S(1)}, u32[]{:S(2)}, u32[]{:S(2)}) collective-permute-start(f32[128,3,512]{2,0,1:T(8,128)S(1)} %get-tuple-element.13), channel_id=1, source_target_pairs={{0,2},{2,4},{4,6},{6,8},{8,10},{10,12},{12,14},{1,3},{3,5},{5,7},{... | collective-permute-start | bytes 2359304 | tf_op jit(solution)/shard_map/ppermute | solution.py:14
  233.1 6.5 %copy-start.2 = (bf16[128,4,512]{2,1,0:T(4,128)(2,1)S(1)}, bf16[128,4,512]{2,1,0:T(4,128)(2,1)}, u32[]{:S(2)}) copy-start(bf16[128,4,512]{2,1,0:T(4,128)(2,1)} %param.14) | copy-start | bytes 1572868
  233.1 6.5 %copy-start.3 = (f32[128,4,512]{2,1,0:T(4,128)S(1)}, f32[128,4,512]{2,1,0:T(4,128)}, u32[]{:S(2)}) copy-start(f32[128,4,512]{2,1,0:T(4,128)} %reshape.53) | copy-start | bytes 3145732
  233.1 6.5 %copy-start.5 = (f32[128,4,512]{2,0,1:T(8,128)S(1)}, f32[128,4,512]{2,0,1:T(8,128)}, u32[]{:S(2)}) copy-start(f32[128,4,512]{2,0,1:T(8,128)} %reduce-scatter.2.cloned.1.call-done) | copy-start | bytes 3145732
  233.1 4.5 %collective-permute-start.6 = (f32[3,10,512]{2,0,1:T(4,128)S(1)}, f32[3,10,512]{2,0,1:T(4,128)S(1)}, u32[]{:S(2)}, u32[]{:S(2)}) collective-permute-start(f32[3,10,512]{2,0,1:T(4,128)S(1)} %get-tuple-element.9), channel_id=1, source_target_pairs={{0,1},{2,3},{4,5},{6,7},{8,9},{10,11},{12,13},{14,15},{16,17},{18,... | collective-permute-start | bytes 184328 | tf_op jit(solution)/shard_map/ppermute | solution.py:14
  234.5 3.9 %collective-permute-start.7 = (f32[3,10,512]{2,0,1:T(4,128)S(1)}, f32[3,10,512]{2,0,1:T(4,128)S(1)}, u32[]{:S(2)}, u32[]{:S(2)}) collective-permute-start(f32[3,10,512]{2,0,1:T(4,128)S(1)} %get-tuple-element.10), channel_id=1, source_target_pairs={{1,0},{3,2},{5,4},{7,6},{9,8},{11,10},{13,12},{15,14},{17,16},{19,... | collective-permute-start | bytes 184328 | tf_op jit(solution)/shard_map/ppermute | solution.py:17
Sparse Core Ops, SparseCore 0:
  132.3 11.7 reduce-scatter.1
where the time goes:
time: 259 us; the launch traced here: 258 us
  waiting for transfers between devices  127 us (49%)
  other arithmetic  38.8 us (15%)
  local copies, waits for them, and re-layouts  29.6 us (11%)
  starting transfers between devices  26.2 us (10%)
  matrix products  23.3 us (9%)
  between operations  13.8 us (5%)
    ppermute x4, waiting for transfers between devices, with_halo(): lax.ppermute(lax.slice_in_dim(block, block.shape[dim] - width, None, axis...  99.7 us
    ppermute x4, waiting for transfers between devices, with_halo(): lax.ppermute(lax.slice_in_dim(block, 0, width, axis=dim), axis, backward)  27.1 us
    reduce_sum x1, other arithmetic, on_device(): mean_val = jnp.mean(conv_out, axis=-1, keepdims=True)  21.4 us
    ppermute x4, starting transfers between devices, with_halo(): lax.ppermute(lax.slice_in_dim(block, block.shape[dim] - width, None, axis...  10.8 us
    add x1, other arithmetic, on_device(): return mismatch + depthwise(d_padded, dw_kernel[::-1, ::-1], tile_v, tile_u)  10.3 us
    dot_general x1, matrix products, on_device(): jnp.dot(activated, w_out, preferred_element_type=jnp.float32) + b_out  10.1 us
    ppermute x4, starting transfers between devices, with_halo(): lax.ppermute(lax.slice_in_dim(block, 0, width, axis=dim), axis, backward)  9.55 us
    dot_general x1, matrix products, on_device(): jnp.dot(d_hidden, w_in.T, preferred_element_type=jnp.float32)  7.04 us
  transfers between devices with their start and end apart: 10, of which 4 were waited for; matrix products, arithmetic and copies ran while one was open for 19% of the time, Pallas kernels for 0%

commit v1 on v0

--- a/solution.py
+++ b/solution.py
@@ -56,7 +56,10 @@
     grid_u = tile_u * row_count
     local_lines = teacher.shape[0] // grid_u
     raw_tokens = teacher.reshape(local_lines, grid_u, teacher.shape[1])
-    arrived = lax.all_to_all(raw_tokens, "row", split_axis=1, concat_axis=0, tiled=True)
+    arrived = jnp.concatenate(
+        lax.all_to_all(jnp.stack(jnp.split(raw_tokens, lax.axis_size("row"), axis=1)), "row", 0, 0),
+        axis=0,
+    )
     partial_value = jnp.dot(
         arrived.reshape(-1, arrived.shape[2]), proj_weight, preferred_element_type=jnp.float32
     )

time: 259 us -> 264 us (1.019)
  local copies, waits for them, and re-layouts: 29.6 us -> 34.9 us
    unnamed x37 -> x46, local copies, waits for them, and re-layouts: 4.47 us -> 11.7 us
    reshape x1 -> x0, local copies, waits for them, and re-layouts: 6.67 us -> none  [on_device(): raw_tokens = teacher.reshape(local_lines, grid_u, teacher.shape[1])]
    another operation x0 -> x2, local copies, waits for them, and re-layouts: none -> 4.77 us  [on_device(): jnp.stack(jnp.split(raw_tokens, lax.axis_size('row'), axis=1))]
where the time goes in v1:
time: 264 us
  waiting for transfers between devices  127 us (48%)
  other arithmetic  38.5 us (15%)
  local copies, waits for them, and re-layouts  34.9 us (13%)
  starting transfers between devices  26.2 us (10%)
  matrix products  23.3 us (9%)
  between operations  13.8 us (5%)
    ppermute x4, waiting for transfers between devices, with_halo(): lax.ppermute(lax.slice_in_dim(block, block.shape[dim] - width, None, axis...  99.8 us
    ppermute x4, waiting for transfers between devices, with_halo(): lax.ppermute(lax.slice_in_dim(block, 0, width, axis=dim), axis, backward)  27 us
    reduce_sum x1, other arithmetic, on_device(): mean_val = jnp.mean(conv_out, axis=-1, keepdims=True)  21.2 us
    unnamed x46, local copies, waits for them, and re-layouts  11.7 us
    ppermute x4, starting transfers between devices, with_halo(): lax.ppermute(lax.slice_in_dim(block, block.shape[dim] - width, None, axis...  10.8 us
    add x1, other arithmetic, on_device(): return mismatch + depthwise(d_padded, dw_kernel[::-1, ::-1], tile_v, tile_u)  10.3 us
    dot_general x1, matrix products, on_device(): jnp.dot(activated, w_out, preferred_element_type=jnp.float32) + b_out  10.1 us
    ppermute x4, starting transfers between devices, with_halo(): lax.ppermute(lax.slice_in_dim(block, 0, width, axis=dim), axis, backward)  9.55 us
  transfers between devices with their start and end apart: 10, of which 4 were waited for; matrix products, arithmetic and copies ran while one was open for 19% of the time, Pallas kernels for 0%

profile of v1, /device:TPU:11, one launch (start us, length us, event | category | flops | bytes accessed | tf_op | source)
XLA Modules:
  0.0 263.6 jit_solution(5399488344864434957)
XLA Ops:
  6.5 1.6 fusion.157
  8.2 1.7 fusion.156
  9.8 1.5 fusion.155
  11.3 1.6 fusion.154
  12.9 0.3 fusion.153
  13.2 0.3 fusion.152
  13.5 0.3 fusion.151
  13.8 0.3 fusion.150
  14.2 4.4 %copy.70 = bf16[8,32,4,2048]{3,1,2,0:T(8,128)(2,1)} copy(bf16[8,32,4,2048]{3,2,1,0:T(4,128)(2,1)S(1)} %fusion.150) | data formatting | bytes 8388608 | tf_op jit(solution)/shard_map/stack | solution.py:60
  18.6 5.8 %all-to-all-start = ((bf16[8,32,4,2048]{3,1,2,0:T(8,128)(2,1)}), bf16[8,32,4,2048]{3,1,2,0:T(8,128)(2,1)}, u32[]{:S(2)}, u32[]{:S(2)}) async-start(bf16[8,32,4,2048]{3,1,2,0:T(8,128)(2,1)} %copy.70), calls=%async_computation | async-start | bytes 8388608 | tf_op jit(solution)/shard_map/all_to_all | solution.py:60
  24.4 0.4 fusion.197
  24.9 3.1 %collective-permute-start = (bf16[128,3,512]{2,0,1:T(8,128)(2,1)S(1)}, bf16[128,3,512]{2,0,1:T(8,128)(2,1)S(1)}, u32[]{:S(2)}, u32[]{:S(2)}) collective-permute-start(bf16[128,3,512]{2,0,1:T(8,128)(2,1)S(1)} %copy.94), channel_id=1, source_target_pairs={{0,2},{2,4},{4,6},{6,8},{8,10},{10,12},{12,14},{1,3},{3,5},{5,7},{... | collective-permute-start | bytes 1179656 | tf_op jit(solution)/shard_map/ppermute | solution.py:14
  28.1 2.2 collective-permute-start.1
  30.4 93.0 %collective-permute-done = bf16[128,3,512]{2,0,1:T(8,128)(2,1)S(1)} collective-permute-done((bf16[128,3,512]{2,0,1:T(8,128)(2,1)S(1)}, bf16[128,3,512]{2,0,1:T(8,128)(2,1)S(1)}, u32[]{:S(2)}, u32[]{:S(2)}) %collective-permute-start) | collective-permute-done | bytes 393248 | tf_op jit(solution)/shard_map/ppermute | solution.py:14
  123.4 1.0 constant_dynamic-update-slice_fusion.3
  124.4 0.9 copy-done.4
  125.4 0.8 constant_dynamic-update-slice_fusion.5
  126.2 1.1 copy-done.8
  127.3 2.4 collective-permute-start.3
  129.7 1.3 collective-permute-start.2
  131.1 2.6 %copy.71 = bf16[8,32,4,2048]{3,1,0,2:T(8,128)(2,1)S(1)} copy(bf16[8,32,4,2048]{3,1,2,0:T(8,128)(2,1)} %all-to-all-done) | data formatting | bytes 8388608 | tf_op jit(solution)/shard_map/all_to_all | solution.py:60
  133.9 3.7 %fusion.16 = f32[256,4,512]{2,0,1:T(8,128)} fusion(bf16[256,4,2048]{2,0,1:T(8,128)(2,1)S(1)} %bitcast.101, bf16[2048,512]{1,0:T(8,128)(2,1)S(1)} %copy-done.14), kind=kOutput, calls=%fused_computation.76 | convolution fusion | flops 2147483648 | bytes 8388608 | tf_op jit(solution)/shard_map/dot_general | solution.py:63
  137.7 21.2 %fusion.193 = (f32[128,4]{0,1:T(4,128)S(1)}, f32[128,4,512]{2,0,1:T(8,128)S(1)}) fusion(f32[512]{0:T(512)S(1)} %copy-done.12, bf16[3,10,512]{2,0,1:T(4,128)(2,1)S(1)} %collective-permute-done.3, bf16[128,10,512]{2,0,1:T(8,128)(2,1)} %copy-done.8, f32[512]{0:T(512)S(1)} %bitcast.158, f32[512]{0:T(512)S(1)} %bitcast.160, f32[512]{0:T(512)S(1)} %bitcast.104, ...), kind=kLoop, calls=%fused_computation.359 | loop fusion | flops 71826944 | bytes 6195200 | tf_op jit(solution)/shard_map/reduce_sum | solution.py:72
  158.9 0.3 multiply_reduce_fusion.2
  159.2 0.2 add_convert_fusion
  159.4 1.2 copy.68
  160.6 2.0 reshape.50
  162.6 2.4 fusion.201
  165.1 1.9 copy-done.7
  167.0 10.1 %fusion.20 = f32[512,512]{1,0:T(8,128)} fusion(bf16[2048,512]{1,0:T(8,128)(2,1)S(1)} %copy-done.15, f32[512,2048]{1,0:T(8,128)S(1)} %fusion.201, f32[2048]{0:T(1024)S(1)} %copy-done.16, f32[512]{0:T(512)S(1)} %copy-done.17), kind=kOutput, calls=%fused_computation.79 | convolution fusion | flops 1143209984 | bytes 7350272 | tf_op jit(solution)/shard_map/dot_general | solution.py:80
  177.1 2.6 reshape.51
  179.8 2.1 multiply_convert_fusion
  181.9 1.2 copy.72
  183.1 2.0 reshape.53
  185.0 7.0 %multiply_reduce_fusion.1 = (f32[512]{0:T(512)S(1)}, f32[512,512]{1,0:T(8,128)}) fusion(f32[512]{0:T(512)S(1)} %copy-done.10, bf16[512,2048]{1,0:T(8,128)(2,1)S(1)} %copy-done, f32[512,2048]{1,0:T(8,128)} %copy-done.7, bf16[512,512]{1,0:T(8,128)(2,1)} %reshape.53, bf16[2048,512]{1,0:T(8,128)(2,1)} %param.21, f32[2048]{0:T(1024)S(1)} %copy-done.16), kind=kOutput, calls=%fused_computation.216 | convolution fusion | flops 2159541760 | bytes 9973760 | tf_op jit(solution)/shard_map/dot_general | solution.py:86
  192.1 2.5 reshape.54
  194.6 1.7 multiply_reduce_fusion
  196.5 1.7 subtract_multiply_fusion
  198.4 1.9 collective-permute-start.5
  200.3 5.0 %collective-permute-start.4 = (f32[128,3,512]{2,0,1:T(8,128)S(1)}, f32[128,3,512]{2,0,1:T(8,128)S(1)}, u32[]{:S(2)}, u32[]{:S(2)}) collective-permute-start(f32[128,3,512]{2,0,1:T(8,128)S(1)} %get-tuple-element.13), channel_id=1, source_target_pairs={{0,2},{2,4},{4,6},{6,8},{8,10},{10,12},{12,14},{1,3},{3,5},{5,7},{... | collective-permute-start | bytes 2359304 | tf_op jit(solution)/shard_map/ppermute | solution.py:14
  205.3 26.1 %collective-permute-done.5 = f32[128,3,512]{2,0,1:T(8,128)S(1)} collective-permute-done((f32[128,3,512]{2,0,1:T(8,128)S(1)}, f32[128,3,512]{2,0,1:T(8,128)S(1)}, u32[]{:S(2)}, u32[]{:S(2)}) %collective-permute-start.5) | collective-permute-done | bytes 786464 | tf_op jit(solution)/shard_map/ppermute | solution.py:17
  231.5 6.8 %collective-permute-done.4 = f32[128,3,512]{2,0,1:T(8,128)S(1)} collective-permute-done((f32[128,3,512]{2,0,1:T(8,128)S(1)}, f32[128,3,512]{2,0,1:T(8,128)S(1)}, u32[]{:S(2)}, u32[]{:S(2)}) %collective-permute-start.4) | collective-permute-done | bytes 786464 | tf_op jit(solution)/shard_map/ppermute | solution.py:14
  238.3 1.4 collective-permute-start.6
  239.8 3.0 %collective-permute-start.7 = (f32[3,10,512]{2,0,1:T(4,128)S(1)}, f32[3,10,512]{2,0,1:T(4,128)S(1)}, u32[]{:S(2)}, u32[]{:S(2)}) collective-permute-start(f32[3,10,512]{2,0,1:T(4,128)S(1)} %get-tuple-element.10), channel_id=1, source_target_pairs={{1,0},{3,2},{5,4},{7,6},{9,8},{11,10},{13,12},{15,14},{17,16},{19,... | collective-permute-start | bytes 184328 | tf_op jit(solution)/shard_map/ppermute | solution.py:17
  242.8 0.9 collective-permute-done.7
  243.7 1.0 maximum_maximum_fusion
  244.8 10.3 %fusion.85 = f32[128,4,512]{2,0,1:T(8,128)S(1)} fusion(f32[131,10,512]{2,0,1:T(8,128)S(1)} %get-tuple-element.8, f32[128,3,512]{2,0,1:T(8,128)S(1)} %collective-permute-done.5, f32[128,4,512]{2,0,1:T(8,128)S(1)} %subtract_multiply_fusion, f32[128,3,512]{2,0,1:T(8,128)S(1)} %collective-permute-done.4, f32[131,10,512]{2,0,1:T(8,128)S(1)} %get-tuple-element.7, ...), kind=kLoop, calls=%fused_computation.145 | loop fusion | flops 28835840 | bytes 50434048 | tf_op jit(solution)/shard_map/add | solution.py:96
  255.1 1.6 copy.75
  (56 shorter events, 1.1 us)
Async XLA Ops:
  6.5 156.1 %copy-start = (bf16[512,2048]{1,0:T(8,128)(2,1)S(1)}, bf16[512,2048]{1,0:T(8,128)(2,1)}, u32[]{:S(2)}) copy-start(bf16[512,2048]{1,0:T(8,128)(2,1)} %param.19) | copy-start | bytes 6291460
  6.5 6.4 %copy-start.5 = (bf16[1024,2048]{1,0:T(8,128)(2,1)S(1)}, bf16[1024,2048]{1,0:T(8,128)(2,1)}, u32[]{:S(2)}) copy-start(bf16[1024,2048]{1,0:T(8,128)(2,1)} %param.12) | copy-start | bytes 12582916
  18.6 5.8 %copy-start.1 = (bf16[128,4,512]{2,1,0:T(4,128)(2,1)S(1)}, bf16[128,4,512]{2,1,0:T(4,128)(2,1)}, u32[]{:S(2)}) copy-start(bf16[128,4,512]{2,1,0:T(4,128)(2,1)} %param.14) | copy-start | bytes 1572868
  18.6 11.7 %copy-start.9 = (f32[7,7,512]{2,1,0:T(8,128)S(1)}, f32[7,7,512]{2,1,0:T(8,128)}, u32[]{:S(2)}) copy-start(f32[7,7,512]{2,1,0:T(8,128)} %param.15) | copy-start | bytes 301060
  18.6 112.4 %all-to-all-start = ((bf16[8,32,4,2048]{3,1,2,0:T(8,128)(2,1)}), bf16[8,32,4,2048]{3,1,2,0:T(8,128)(2,1)}, u32[]{:S(2)}, u32[]{:S(2)}) async-start(bf16[8,32,4,2048]{3,1,2,0:T(8,128)(2,1)} %copy.70), calls=%async_computation | async-start | bytes 8388608 | tf_op jit(solution)/shard_map/all_to_all | solution.py:60
  24.4 155.3 %reduce-scatter.2.cloned.1.call-start = ((), (), s32[]{:S(2)}) async-start(), calls=%async_computation.2 | async-start | bytes 3145728 | tf_op jit(solution)/shard_map/reduce_scatter | solution.py:67
  24.9 98.5 %collective-permute-start = (bf16[128,3,512]{2,0,1:T(8,128)(2,1)S(1)}, bf16[128,3,512]{2,0,1:T(8,128)(2,1)S(1)}, u32[]{:S(2)}, u32[]{:S(2)}) collective-permute-start(bf16[128,3,512]{2,0,1:T(8,128)(2,1)S(1)} %copy.94), channel_id=1, source_target_pairs={{0,2},{2,4},{4,6},{6,8},{8,10},{10,12},{12,14},{1,3},{3,5},{5,7},{... | collective-permute-start | bytes 1179656 | tf_op jit(solution)/shard_map/ppermute | solution.py:14
  28.1 97.3 %collective-permute-start.1 = (bf16[128,3,512]{2,0,1:T(8,128)(2,1)S(1)}, bf16[128,3,512]{2,0,1:T(8,128)(2,1)S(1)}, u32[]{:S(2)}, u32[]{:S(2)}) collective-permute-start(bf16[128,3,512]{2,0,1:T(8,128)(2,1)S(1)} %copy.95), channel_id=1, source_target_pairs={{2,0},{4,2},{6,4},{8,6},{10,8},{12,10},{14,12},{3,1},{5,3},{7,5},{... | collective-permute-start | bytes 1179656 | tf_op jit(solution)/shard_map/ppermute | solution.py:17
  124.4 0.9 copy-start.4
  126.2 1.1 copy-start.8
  127.3 10.3 %collective-permute-start.3 = (bf16[3,10,512]{2,0,1:T(4,128)(2,1)S(1)}, bf16[3,10,512]{2,0,1:T(4,128)(2,1)S(1)}, u32[]{:S(2)}, u32[]{:S(2)}) collective-permute-start(bf16[3,10,512]{2,0,1:T(4,128)(2,1)S(1)} %get-tuple-element.12), channel_id=1, source_target_pairs={{1,0},{3,2},{5,4},{7,6},{9,8},{11,10},{13,12},{15,14},{17,16},{19,... | collective-permute-start | bytes 92168 | tf_op jit(solution)/shard_map/ppermute | solution.py:17
  129.7 7.9 %collective-permute-start.2 = (bf16[3,10,512]{2,0,1:T(4,128)(2,1)S(1)}, bf16[3,10,512]{2,0,1:T(4,128)(2,1)S(1)}, u32[]{:S(2)}, u32[]{:S(2)}) collective-permute-start(bf16[3,10,512]{2,0,1:T(4,128)(2,1)S(1)} %get-tuple-element.11), channel_id=1, source_target_pairs={{0,1},{2,3},{4,5},{6,7},{8,9},{10,11},{12,13},{14,15},{16,17},{18,... | collective-permute-start | bytes 92168 | tf_op jit(solution)/shard_map/ppermute | solution.py:14
  131.0 2.9 %copy-start.14 = (bf16[2048,512]{1,0:T(8,128)(2,1)S(1)}, bf16[2048,512]{1,0:T(8,128)(2,1)}, u32[]{:S(2)}) copy-start(bf16[2048,512]{1,0:T(8,128)(2,1)} %param.13) | copy-start | bytes 6291460
  133.9 3.8 %copy-start.12 = (f32[512]{0:T(512)S(1)}, f32[512]{0:T(512)}, u32[]{:S(2)}) copy-start(f32[512]{0:T(512)} %param.16) | copy-start | bytes 6148
  137.6 21.5 %copy-start.10 = (f32[512]{0:T(512)S(1)}, f32[512]{0:T(512)}, u32[]{:S(2)}) copy-start(f32[512]{0:T(512)} %param.17) | copy-start | bytes 6148
  137.6 21.5 %copy-start.13 = (f32[512]{0:T(512)S(1)}, f32[512]{0:T(512)}, u32[]{:S(2)}) copy-start(f32[512]{0:T(512)} %param.18) | copy-start | bytes 6148
  160.6 6.4 %copy-start.16 = (f32[2048]{0:T(1024)S(1)}, f32[2048]{0:T(1024)}, u32[]{:S(2)}) copy-start(f32[2048]{0:T(1024)} %param.20) | copy-start | bytes 24580
  160.6 6.4 %copy-start.17 = (f32[512]{0:T(512)S(1)}, f32[512]{0:T(512)}, u32[]{:S(2)}) copy-start(f32[512]{0:T(512)} %param.22) | copy-start | bytes 6148
  162.6 4.4 %copy-start.15 = (bf16[2048,512]{1,0:T(8,128)(2,1)S(1)}, bf16[2048,512]{1,0:T(8,128)(2,1)}, u32[]{:S(2)}) copy-start(bf16[2048,512]{1,0:T(8,128)(2,1)} %param.21) | copy-start | bytes 6291460
  165.1 2.0 copy-start.7
  167.0 12.7 %copy-start.11 = (f32[512]{0:T(512)S(1)}, f32[512]{0:T(512)}, u32[]{:S(2)}) copy-start(f32[512]{0:T(512)} %param.23) | copy-start | bytes 6148
  198.4 33.1 %collective-permute-start.5 = (f32[128,3,512]{2,0,1:T(8,128)S(1)}, f32[128,3,512]{2,0,1:T(8,128)S(1)}, u32[]{:S(2)}, u32[]{:S(2)}) collective-permute-start(f32[128,3,512]{2,0,1:T(8,128)S(1)} %get-tuple-element.14), channel_id=1, source_target_pairs={{2,0},{4,2},{6,4},{8,6},{10,8},{12,10},{14,12},{3,1},{5,3},{7,5},{... | collective-permute-start | bytes 2359304 | tf_op jit(solution)/shard_map/ppermute | solution.py:17
  200.3 38.0 %collective-permute-start.4 = (f32[128,3,512]{2,0,1:T(8,128)S(1)}, f32[128,3,512]{2,0,1:T(8,128)S(1)}, u32[]{:S(2)}, u32[]{:S(2)}) collective-permute-start(f32[128,3,512]{2,0,1:T(8,128)S(1)} %get-tuple-element.13), channel_id=1, source_target_pairs={{0,2},{2,4},{4,6},{6,8},{8,10},{10,12},{12,14},{1,3},{3,5},{5,7},{... | collective-permute-start | bytes 2359304 | tf_op jit(solution)/shard_map/ppermute | solution.py:14
  238.3 6.5 %copy-start.2 = (bf16[128,4,512]{2,1,0:T(4,128)(2,1)S(1)}, bf16[128,4,512]{2,1,0:T(4,128)(2,1)}, u32[]{:S(2)}) copy-start(bf16[128,4,512]{2,1,0:T(4,128)(2,1)} %param.14) | copy-start | bytes 1572868
  238.3 6.5 %copy-start.3 = (f32[128,4,512]{2,1,0:T(4,128)S(1)}, f32[128,4,512]{2,1,0:T(4,128)}, u32[]{:S(2)}) copy-start(f32[128,4,512]{2,1,0:T(4,128)} %reshape.51) | copy-start | bytes 3145732
  238.3 6.5 %copy-start.6 = (f32[128,4,512]{2,0,1:T(8,128)S(1)}, f32[128,4,512]{2,0,1:T(8,128)}, u32[]{:S(2)}) copy-start(f32[128,4,512]{2,0,1:T(8,128)} %reduce-scatter.2.cloned.1.call-done) | copy-start | bytes 3145732
  238.3 4.5 %collective-permute-start.6 = (f32[3,10,512]{2,0,1:T(4,128)S(1)}, f32[3,10,512]{2,0,1:T(4,128)S(1)}, u32[]{:S(2)}, u32[]{:S(2)}) collective-permute-start(f32[3,10,512]{2,0,1:T(4,128)S(1)} %get-tuple-element.9), channel_id=1, source_target_pairs={{0,1},{2,3},{4,5},{6,7},{8,9},{10,11},{12,13},{14,15},{16,17},{18,... | collective-permute-start | bytes 184328 | tf_op jit(solution)/shard_map/ppermute | solution.py:14
  239.8 3.9 %collective-permute-start.7 = (f32[3,10,512]{2,0,1:T(4,128)S(1)}, f32[3,10,512]{2,0,1:T(4,128)S(1)}, u32[]{:S(2)}, u32[]{:S(2)}) collective-permute-start(f32[3,10,512]{2,0,1:T(4,128)S(1)} %get-tuple-element.10), channel_id=1, source_target_pairs={{1,0},{3,2},{5,4},{7,6},{9,8},{11,10},{13,12},{15,14},{17,16},{19,... | collective-permute-start | bytes 184328 | tf_op jit(solution)/shard_map/ppermute | solution.py:17
Sparse Core Ops, SparseCore 0:
  137.7 11.7 reduce-scatter.1
